TPU v7x, 256 devices: a whole 4x4x8 slice. The times are simulated.
256 devices in a mesh: shard: 32 (over z, y), dp: 8 (over x, core).
Axes of the slice: x: 4, y: 4, z: 8, core: 2. Of those that a mesh axis runs over, the one named last changes fastest.
Arguments:
- cold_table: bfloat16 [65536, 256], P('shard'), may hold values from -6 to 6
- cold_accum: float32 [65536], P('shard'), may hold values from 0.005 to 0.5
- dither_bits: int32 [65536, 256], P('shard'), may hold values from 0 to 65280
- hot_table: float32 [1024, 256], replicated, may hold values from -6 to 6
- hot_accum: float32 [1024], replicated, may hold values from 1 to 100
- w_flat: bfloat16 [4096, 512], replicated, may hold values from -0.09375 to 0.09375
- w_inter: bfloat16 [256, 512], replicated, may hold values from -0.09375 to 0.09375
- hidden_bias: float32 [512], replicated, may hold values from -1 to 1
- w_out: float32 [512], replicated, may hold values from -0.25 to 0.25
- targets: float32 [131072], P(('shard', 'dp')), may hold values from 0 to 1
- hot_ids: int32 [131072, 8], P(('shard', 'dp')), may hold values from 0 to 1023
- cold_slots: int32 [131072, 8], P(('shard', 'dp')), may hold values from 0 to 2047, as said below
- requests: int32 [16384, 64], P(('shard', 'dp')), may hold values from 0 to 2047, as said below
- counts: int32 [512, 32], P(('shard', 'dp')), may hold values from 1 to 64, as said below
Outputs:
- cold_out: bfloat16 [65536, 256], P('shard')
- cold_accum_out: float32 [65536], P('shard')
- hot_out: float32 [1024, 256], replicated
- hot_accum_out: float32 [1024], replicated
Inputs may be any that keep to these rules, and one draw needn't show every extreme that they name: `requests`: in each row of 64 entries (one device, micro-batch and shard) the entries name distinct rows of that shard's 2048; only the first counts-many are live, the rest name arbitrary rows. `counts`: in every draw, each device has in each micro-batch a shard with exactly 64 live slots. `cold_slots`: index into its device's request rows of that micro-batch, shard * 64 + slot; always a live slot, and every live slot is named by some lookup.
All inputs are finite; a program needn't handle non-finite values.
Results may differ from a plain program's by a relative error of at most 0.001.
The roundings to bfloat16 on the way count: a program that leaves them out, or rounds other values in their place, can miss the bound.
Values may be sent and summed in bfloat16 or wider, within the bound.
No kernel may reach another device: no remote copies, remote signals or barrier semaphores. Data moves between devices by JAX's collectives and lax.ppermute only.
A program may use at most 128 MiB of HBM per device.

v0:
```python
import jax
import jax.numpy as jnp
from jax import lax
from jax.sharding import PartitionSpec as P

MB = 2
BATCH = 256
learn_rate = 0.3


def backprop(stacked, targets, w_flat, w_inter, hidden_bias, w_out):
    row_count, feature_count, row_width = stacked.shape
    flattened = stacked.reshape(row_count, feature_count * row_width)
    pair_dots = (
        jnp.einsum("sfe,sge->sfg", stacked, stacked, preferred_element_type=jnp.float32)
        * row_width ** (-0.5)
    ).astype(jnp.bfloat16)
    pre_act = jnp.dot(flattened, w_flat, preferred_element_type=jnp.float32)
    pre_act = pre_act + jnp.dot(
        pair_dots.reshape(row_count, feature_count * feature_count),
        w_inter,
        preferred_element_type=jnp.float32,
    )
    pre_act = pre_act + hidden_bias
    gated = jax.nn.sigmoid(pre_act)
    logits = jnp.sum(pre_act * gated * w_out, axis=-1)
    residual = jax.nn.sigmoid(logits) - targets
    slopes = (residual[:, None] * w_out * gated * (1.0 + pre_act * (1.0 - gated))).astype(
        jnp.bfloat16
    )
    back_flat = jnp.dot(slopes, w_flat.T, preferred_element_type=jnp.float32)
    back_pairs = jnp.dot(slopes, w_inter.T, preferred_element_type=jnp.float32).reshape(
        row_count, feature_count, feature_count
    )
    mirror = ((back_pairs + jnp.swapaxes(back_pairs, 1, 2)) * row_width ** (-0.5)).astype(
        jnp.bfloat16
    )
    return back_flat.reshape(row_count, feature_count, row_width) + jnp.einsum(
        "sfg,sge->sfe", mirror, stacked, preferred_element_type=jnp.float32
    )


def adagrad_rows(table_rows, accum, gradient):
    accum_new = accum + jnp.mean(gradient * gradient, axis=-1)
    updated = table_rows - learn_rate * gradient / jnp.sqrt(accum_new)[:, None]
    return (updated, accum_new)


def requantize(updated, bits, touched):
    grid_step = jnp.max(jnp.abs(updated), axis=-1, keepdims=True) / 8.0
    dither = bits.astype(jnp.float32) * (1.0 / 65280.0) - 0.5
    return jnp.where(touched[:, None], updated + grid_step * dither, updated).astype(jnp.bfloat16)


def on_device(
    cold_table,
    cold_accum,
    dither_bits,
    hot_table,
    hot_accum,
    w_flat,
    w_inter,
    hidden_bias,
    w_out,
    targets,
    hot_ids,
    cold_slots,
    requests,
    counts,
):
    shards = lax.axis_size("shard")
    capacity = requests.shape[1]
    row_count = cold_table.shape[0]
    row_width = cold_table.shape[1]
    hot_count = hot_table.shape[0]
    cold_feats = cold_slots.shape[1]
    hot_grad = jnp.zeros((hot_count, row_width), jnp.float32)
    cold_grad = jnp.zeros((row_count, row_width), jnp.float32)
    touched = jnp.zeros((row_count,), jnp.float32)
    for micro_index in range(MB):
        asked_rows = requests[micro_index * shards : (micro_index + 1) * shards]
        requested = lax.all_to_all(asked_rows, "shard", split_axis=0, concat_axis=0, tiled=True)
        fetched_rows = lax.all_to_all(
            cold_table[requested], "shard", split_axis=0, concat_axis=0, tiled=True
        )
        first = micro_index * BATCH
        slot_part = cold_slots[first : first + BATCH]
        hot_part = hot_ids[first : first + BATCH]
        cold_vectors = fetched_rows.reshape(shards * capacity, row_width)[slot_part]
        stacked = jnp.concatenate([cold_vectors, hot_table[hot_part].astype(jnp.bfloat16)], axis=1)
        gradients = backprop(
            stacked, targets[first : first + BATCH], w_flat, w_inter, hidden_bias, w_out
        )
        slot_grad = jax.ops.segment_sum(
            gradients[:, :cold_feats].reshape(-1, row_width),
            slot_part.reshape(-1),
            num_segments=shards * capacity,
        )
        hot_term = jax.ops.segment_sum(
            gradients[:, cold_feats:].reshape(-1, row_width),
            hot_part.reshape(-1),
            num_segments=hot_count,
        )
        slot_grad, hot_term = (slot_grad.reshape(shards, capacity, row_width), hot_term)
        hot_grad = hot_grad + hot_term
        owner_grad, count_in = (
            lax.all_to_all(
                slot_grad.astype(jnp.bfloat16), "shard", split_axis=0, concat_axis=0, tiled=True
            ).astype(slot_grad.dtype),
            lax.all_to_all(counts[micro_index], "shard", split_axis=0, concat_axis=0, tiled=True),
        )
        cold_grad = cold_grad + jax.ops.segment_sum(
            owner_grad.reshape(-1, row_width), requested.reshape(-1), num_segments=row_count
        )
        live_mask = (jnp.arange(capacity, dtype=jnp.int32)[None, :] < count_in[:, None]).astype(
            jnp.float32
        )
        touched = touched + jax.ops.segment_sum(
            live_mask.reshape(-1), requested.reshape(-1), num_segments=row_count
        )
    summed_grad, summed_hits = (
        lax.psum(cold_grad.astype(jnp.bfloat16), "dp").astype(jnp.float32),
        lax.psum(touched.astype(jnp.bfloat16), "dp").astype(jnp.float32),
    )
    averaged = summed_grad / jnp.maximum(summed_hits, 1.0)[:, None]
    updated, cold_accum_out = adagrad_rows(cold_table.astype(jnp.float32), cold_accum, averaged)
    cold_out = requantize(updated, dither_bits, summed_hits > 0.5)
    total_hot = lax.psum(hot_grad, ("shard", "dp"))
    hot_out, hot_accum_out = adagrad_rows(hot_table, hot_accum, total_hot)
    return (cold_out, cold_accum_out, hot_out, hot_accum_out)


def solution(mesh):
    return jax.shard_map(
        on_device,
        mesh=mesh,
        in_specs=(
            P("shard", None),
            P("shard"),
            P("shard", None),
            P(),
            P(),
            P(),
            P(),
            P(),
            P(),
            P(("shard", "dp")),
            P(("shard", "dp"), None),
            P(("shard", "dp"), None),
            P(("shard", "dp"), None),
            P(("shard", "dp"), None),
        ),
        out_specs=(P("shard", None), P("shard"), P(), P()),
        check_vma=False,
    )
```

profile of v0, /device:TPU:8, one launch (start us, length us, event | category | flops | bytes accessed | tf_op | source)
XLA Modules:
  0.0 695.9 jit_solution(9611974366071185003)
XLA Ops:
  8.0 1.4 fusion.31
  9.4 20.0 %all_to_all.62 = s32[32,1,64]{2,1,0:T(1,128)S(1)} all-to-all(s32[32,1,64]{2,1,0:T(1,128)S(1)} %bitcast.113), channel_id=1, replica_groups=mesh['shard'=32,'dp'=8] {'shard'}, dimensions={0} | all-to-all | bytes 16384 | tf_op jit(solution)/shard_map/all_to_all | solution.py:82
  29.4 4.9 all-to-all-start
  34.5 9.9 %gather_fusion.3 = bf16[2048,256]{1,0:T(8,128)(2,1)} fusion(bf16[2048,256]{1,0:T(8,128)(2,1)} %param.14, s32[2048]{0:T(1024)S(1)} %broadcast_clamp_fusion.3), kind=kCustom, calls=%fused_computation.3 | custom fusion | bytes 2105344 | tf_op jit(solution)/shard_map/gather | solution.py:84
  44.3 10.0 %all-to-all-start.6 = ((bf16[32,64,256]{2,1,0:T(8,128)(2,1)}), bf16[32,64,256]{2,1,0:T(8,128)(2,1)S(1)}, u32[]{:S(2)}, u32[]{:S(2)}) async-start(bf16[32,64,256]{2,1,0:T(8,128)(2,1)} %bitcast.16), calls=%async_computation.6 | async-start | bytes 2097152 | tf_op jit(solution)/shard_map/all_to_all | solution.py:83
  54.5 9.1 %gather_fusion = bf16[2048,256]{1,0:T(8,128)(2,1)} fusion(bf16[2048,256]{1,0:T(8,128)(2,1)S(1)} %copy-done.2, s32[2048]{0:T(1024)S(1)} %broadcast_clamp_fusion.5), kind=kCustom, calls=%fused_computation | custom fusion | bytes 2105344 | tf_op jit(solution)/shard_map/gather | solution.py:84
  63.5 17.2 %all-to-all-done.6 = bf16[32,64,256]{2,1,0:T(8,128)(2,1)S(1)} async-done(((bf16[32,64,256]{2,1,0:T(8,128)(2,1)}), bf16[32,64,256]{2,1,0:T(8,128)(2,1)S(1)}, u32[]{:S(2)}, u32[]{:S(2)}) %all-to-all-start.6) | async-done | bytes 1048608 | tf_op jit(solution)/shard_map/all_to_all | solution.py:83
  80.7 5.6 all-to-all-start.4
  88.4 0.8 copy.69
  89.9 0.8 copy.75
  93.0 1.3 fusion.32
  94.3 0.8 copy.70
  98.1 8.4 %gather_fusion.5 = bf16[2048,256]{1,0:T(8,128)(2,1)} fusion(f32[1024,256]{1,0:T(8,128)S(1)} %copy-done.1, s32[2048]{0:T(1024)S(1)} %broadcast_clamp_fusion), kind=kCustom, calls=%fused_computation.5 | custom fusion | bytes 2105344 | tf_op jit(solution)/shard_map/gather | solution.py:90
  106.5 8.5 %gather_fusion.2 = bf16[2048,256]{1,0:T(8,128)(2,1)} fusion(f32[1024,256]{1,0:T(8,128)S(1)} %copy-done.1, s32[2048]{0:T(1024)S(1)} %broadcast_clamp_fusion.1), kind=kCustom, calls=%fused_computation.2 | custom fusion | bytes 2105344 | tf_op jit(solution)/shard_map/gather | solution.py:90
  115.0 9.0 %gather_fusion.4 = bf16[2048,256]{1,0:T(8,128)(2,1)} fusion(bf16[2048,256]{1,0:T(8,128)(2,1)S(1)} %bitcast.86, s32[2048]{0:T(1024)S(1)} %broadcast_clamp_fusion.2), kind=kCustom, calls=%fused_computation.4 | custom fusion | bytes 2105344 | tf_op jit(solution)/shard_map/gather | solution.py:89
  124.1 4.4 fusion.27
  128.5 1.5 pad_maximum_fusion.1
  129.9 10.5 %all-to-all-start.3 = ((s32[32,1,1]{2,1,0:T(1,128)}), s32[32,1,1]{2,1,0:T(1,128)}, u32[]{:S(2)}, u32[]{:S(2)}) async-start(s32[32,1,1]{2,1,0:T(1,128)} %copy.67), calls=%async_computation.3 | async-start | bytes 32768 | tf_op jit(solution)/shard_map/all_to_all | solution.py:110
  140.5 9.9 %gather_fusion.1 = bf16[2048,256]{1,0:T(8,128)(2,1)} fusion(bf16[2048,256]{1,0:T(8,128)(2,1)} %bitcast.6, s32[2048]{0:T(1024)S(1)} %broadcast_clamp_fusion.4), kind=kCustom, calls=%fused_computation.1 | custom fusion | bytes 2105344 | tf_op jit(solution)/shard_map/gather | solution.py:89
  150.3 4.3 fusion.28
  154.7 1.5 pad_maximum_fusion
  156.2 3.2 copy.77
  159.4 1.0 multiply_convert_fusion.2
  160.4 3.9 copy.84
  164.2 3.2 copy.71
  167.4 1.0 multiply_convert_fusion.3
  168.4 2.7 copy.82
  171.2 2.8 fusion.37
  174.1 1.2 fusion.34
  176.3 1.0 multiply_convert_fusion
  177.6 3.2 fusion.35
  181.0 1.9 copy.73
  182.8 5.9 copy.83
  188.7 10.1 %all-to-all-start.1 = ((s32[32,1,1]{2,1,0:T(1,128)}), s32[32,1,1]{2,1,0:T(1,128)S(1)}, u32[]{:S(2)}, u32[]{:S(2)}) async-start(s32[32,1,1]{2,1,0:T(1,128)} %copy.66), calls=%async_computation.1 | async-start | bytes 32768 | tf_op jit(solution)/shard_map/all_to_all | solution.py:110
  198.8 5.8 bitcast_add_fusion.1
  204.6 13.5 %scatter_custom_fusion.2 = f32[2048,256]{1,0:T(8,128)} fusion(s32[2048]{0:T(1024)} %reshape.252, f32[256,16,256]{2,1,0:T(8,128)} %bitcast_add_fusion.1, f32[]{:T(128)} %constant.13.clone.1), kind=kCustom, calls=%fused_computation.25 | custom fusion | flops 524288 | bytes 4194816 | tf_op jit(solution)/shard_map/scatter-add | solution.py:94
  218.1 2.7 convert_element_type.84
  220.8 9.8 %all-to-all-start.5 = ((bf16[32,64,256]{2,1,0:T(8,128)(2,1)}), bf16[32,64,256]{2,1,0:T(8,128)(2,1)}, u32[]{:S(2)}, u32[]{:S(2)}) async-start(bf16[32,64,256]{2,1,0:T(8,128)(2,1)} %bitcast.104), calls=%async_computation.5 | async-start | bytes 2097152 | tf_op jit(solution)/shard_map/all_to_all | solution.py:107
  230.6 0.8 copy.74
  232.1 1.2 fusion.39
  233.5 1.9 copy.79
  235.4 3.6 fusion.38
  239.0 1.8 copy.85
  240.8 2.9 bitcast_add_fusion
  243.7 13.6 %scatter_custom_fusion.4 = f32[2048,256]{1,0:T(8,128)} fusion(s32[2048]{0:T(1024)} %reshape.268, f32[256,16,256]{2,1,0:T(8,128)} %bitcast_add_fusion, f32[]{:T(128)} %constant.13.clone.1), kind=kCustom, calls=%fused_computation.23 | custom fusion | flops 524288 | bytes 4194816 | tf_op jit(solution)/shard_map/scatter-add | solution.py:94
  257.3 2.7 convert_element_type.90
  260.0 10.0 %all-to-all-start.7 = ((bf16[32,64,256]{2,1,0:T(8,128)(2,1)}), bf16[32,64,256]{2,1,0:T(8,128)(2,1)}, u32[]{:S(2)}, u32[]{:S(2)}) async-start(bf16[32,64,256]{2,1,0:T(8,128)(2,1)} %bitcast.24), calls=%async_computation.7 | async-start | bytes 2097152 | tf_op jit(solution)/shard_map/all_to_all | solution.py:107
  270.7 1.4 reduce.3
  275.1 11.3 %scatter_custom_fusion.1 = f32[2048]{0:T(1024)S(1)} fusion(s32[2048]{0:T(1024)S(1)} %reshape.244, f32[2048]{0:T(1024)S(1)} %reshape.246, f32[]{:T(128)} %constant.13.clone.1), kind=kCustom, calls=%fused_computation.87 | custom fusion | flops 2048 | bytes 8196 | tf_op jit(solution)/shard_map/scatter-add | solution.py:118
  286.4 11.3 %scatter_custom_fusion = f32[2048]{0:T(1024)S(1)} fusion(s32[2048]{0:T(1024)S(1)} %reshape.236, f32[2048]{0:T(1024)S(1)} %reshape.238, f32[]{:T(128)} %constant.13.clone.1), kind=kCustom, calls=%fused_computation.89 | custom fusion | flops 2048 | bytes 8196 | tf_op jit(solution)/shard_map/scatter-add | solution.py:118
  297.7 12.4 %scatter_custom_fusion.6 = f32[1024,256]{1,0:T(8,128)S(1)} fusion(s32[2048]{0:T(1024)S(1)} %reshape.284, f32[256,16,256]{2,1,0:T(8,128)} %bitcast_add_fusion.1, f32[]{:T(128)} %constant.13.clone.1), kind=kCustom, calls=%fused_computation.21 | custom fusion | flops 524288 | bytes 3146240 | tf_op jit(solution)/shard_map/scatter-add | solution.py:99
  310.1 13.1 %scatter_custom_fusion.7 = f32[1024,256]{1,0:T(8,128)} fusion(s32[2048]{0:T(1024)S(1)} %reshape.292, f32[256,16,256]{2,1,0:T(8,128)} %bitcast_add_fusion, f32[]{:T(128)} %constant.13.clone.1), kind=kCustom, calls=%fused_computation.19 | custom fusion | flops 524288 | bytes 3146240 | tf_op jit(solution)/shard_map/scatter-add | solution.py:99
  323.2 2.3 add.148
  325.6 12.4 %psum.21 = bf16[2048]{0:T(1024)(128)(2,1)S(1)} all-reduce(bf16[2048]{0:T(1024)(128)(2,1)S(1)} %add_convert_fusion.1), channel_id=1, replica_groups=mesh['shard'=32,'dp'=8] {'dp'}, use_global_device_ids=true, to_apply=%region_2.0 | all-reduce | flops 2048 | bytes 8192 | tf_op jit(solution)/shard_map/psum | solution.py:123
  338.1 247.5 %all-reduce.5.cloned.1.call-done = f32[1024,256]{1,0:T(8,128)} async-done(((f32[1024,256]{1,0:T(8,128)}), f32[1024,256]{1,0:T(8,128)}) %all-reduce.5.cloned.1.call-update) | async-done | bytes 1048592 | tf_op jit(solution)/shard_map/psum | solution.py:128
  585.6 1.4 multiply_reduce_fusion.1
  587.0 12.6 %scatter_custom_fusion.3 = f32[2048,256]{1,0:T(8,128)} fusion(s32[2048]{0:T(1024)S(1)} %reshape.236, bf16[2048,256]{1,0:T(8,128)(2,1)} %bitcast.28, f32[]{:T(128)} %constant.13.clone.1), kind=kCustom, calls=%fused_computation.30 | custom fusion | flops 1048576 | bytes 3145732 | tf_op jit(solution)/shard_map/scatter-add | solution.py:112
  599.6 12.3 %scatter_custom_fusion.5 = f32[2048,256]{1,0:T(8,128)} fusion(s32[2048]{0:T(1024)S(1)} %reshape.244, bf16[2048,256]{1,0:T(8,128)(2,1)} %bitcast.29, f32[]{:T(128)} %constant.13.clone.1), kind=kCustom, calls=%fused_computation.28 | custom fusion | flops 1048576 | bytes 3145732 | tf_op jit(solution)/shard_map/scatter-add | solution.py:112
  611.9 3.5 add_convert_fusion
  616.1 1.2 divide_subtract_fusion.1
  617.3 64.7 %all-reduce.3.cloned.1.call-done = bf16[2048,256]{1,0:T(8,128)(2,1)} async-done(((bf16[2048,256]{1,0:T(8,128)(2,1)}), bf16[2048,256]{1,0:T(8,128)(2,1)}) %all-reduce.3.cloned.1.call-update) | async-done | bytes 1048592 | tf_op jit(solution)/shard_map/psum | solution.py:122
  681.9 1.9 multiply_reduce_fusion
  684.5 2.2 abs_reduce_fusion
  686.7 1.5 fusion
  (114 shorter events, 15.5 us)
Async XLA Ops:
  8.0 167.3 %copy-start = (bf16[256,512]{1,0:T(8,128)(2,1)S(1)}, bf16[256,512]{1,0:T(8,128)(2,1)}, u32[]{:S(2)}) copy-start(bf16[256,512]{1,0:T(8,128)(2,1)} %param.20) | copy-start | bytes 786436
  29.4 14.9 %copy-start.12 = (s32[32,1,64]{2,1,0:T(1,128)}, s32[32,1,64]{2,1,0:T(1,128)S(1)}, u32[]{:S(2)}) copy-start(s32[32,1,64]{2,1,0:T(1,128)S(1)} %all_to_all.62) | copy-start | bytes 24580
  29.4 14.9 %all-to-all-start = ((s32[32,1,64]{2,1,0:T(1,128)}), s32[32,1,64]{2,1,0:T(1,128)S(1)}, u32[]{:S(2)}, u32[]{:S(2)}) async-start(s32[32,1,64]{2,1,0:T(1,128)} %bitcast), calls=%async_computation | async-start | bytes 32768 | tf_op jit(solution)/shard_map/all_to_all | solution.py:82
  44.3 10.1 %copy-start.2 = (bf16[2048,256]{1,0:T(8,128)(2,1)S(1)}, bf16[2048,256]{1,0:T(8,128)(2,1)}, u32[]{:S(2)}) copy-start(bf16[2048,256]{1,0:T(8,128)(2,1)} %param.14) | copy-start | bytes 3145732
  44.3 36.4 %all-to-all-start.6 = ((bf16[32,64,256]{2,1,0:T(8,128)(2,1)}), bf16[32,64,256]{2,1,0:T(8,128)(2,1)S(1)}, u32[]{:S(2)}, u32[]{:S(2)}) async-start(bf16[32,64,256]{2,1,0:T(8,128)(2,1)} %bitcast.16), calls=%async_computation.6 | async-start | bytes 2097152 | tf_op jit(solution)/shard_map/all_to_all | solution.py:83
  63.5 22.8 %copy-start.27 = (s32[2,32]{1,0:T(2,128)S(1)}, s32[2,32]{1,0:T(2,128)}, u32[]{:S(2)}) copy-start(s32[2,32]{1,0:T(2,128)} %param.27) | copy-start | bytes 772
  63.5 24.2 %copy-start.21 = (s32[512,8]{0,1:T(8,128)S(1)}, s32[512,8]{0,1:T(8,128)}, u32[]{:S(2)}) copy-start(s32[512,8]{0,1:T(8,128)} %param.25) | copy-start | bytes 49156
  63.5 34.5 %copy-start.1 = (f32[1024,256]{1,0:T(8,128)S(1)}, f32[1024,256]{1,0:T(8,128)}, u32[]{:S(2)}) copy-start(f32[1024,256]{1,0:T(8,128)} %param.17) | copy-start | bytes 3145732
  80.7 49.2 %all-to-all-start.4 = ((bf16[32,64,256]{2,1,0:T(8,128)(2,1)}), bf16[32,64,256]{2,1,0:T(8,128)(2,1)}, u32[]{:S(2)}, u32[]{:S(2)}) async-start(bf16[32,64,256]{2,1,0:T(8,128)(2,1)} %bitcast.103), calls=%async_computation.4 | async-start | bytes 2097152 | tf_op jit(solution)/shard_map/all_to_all | solution.py:83
  98.1 8.4 %copy-start.18 = (s32[2048]{0:T(1024)S(1)}, s32[2048]{0:T(1024)}, u32[]{:S(2)}) copy-start(s32[2048]{0:T(1024)} %reshape.204) | copy-start | bytes 24580
  106.5 8.5 %copy-start.16 = (s32[2048]{0:T(1024)S(1)}, s32[2048]{0:T(1024)}, u32[]{:S(2)}) copy-start(s32[2048]{0:T(1024)} %reshape.196) | copy-start | bytes 24580
  106.5 8.5 %copy-start.17 = (s32[2048]{0:T(1024)S(1)}, s32[2048]{0:T(1024)}, u32[]{:S(2)}) copy-start(s32[2048]{0:T(1024)} %reshape.220) | copy-start | bytes 24580
  124.0 4.4 copy-start.4
  124.0 4.4 copy-start.5
  129.9 58.8 %all-to-all-start.3 = ((s32[32,1,1]{2,1,0:T(1,128)}), s32[32,1,1]{2,1,0:T(1,128)}, u32[]{:S(2)}, u32[]{:S(2)}) async-start(s32[32,1,1]{2,1,0:T(1,128)} %copy.67), calls=%async_computation.3 | async-start | bytes 32768 | tf_op jit(solution)/shard_map/all_to_all | solution.py:110
  150.3 4.3 copy-start.7
  150.3 4.3 copy-start.8
  168.4 2.8 copy-start.3
  174.1 1.3 copy-start.24
  174.1 1.5 copy-start.25
  175.6 0.7 copy-start.26
  188.7 32.0 %all-to-all-start.1 = ((s32[32,1,1]{2,1,0:T(1,128)}), s32[32,1,1]{2,1,0:T(1,128)S(1)}, u32[]{:S(2)}, u32[]{:S(2)}) async-start(s32[32,1,1]{2,1,0:T(1,128)} %copy.66), calls=%async_computation.1 | async-start | bytes 32768 | tf_op jit(solution)/shard_map/all_to_all | solution.py:110
  220.8 9.8 %copy-start.14 = (s32[32,1,1]{2,1,0:T(1,128)}, s32[32,1,1]{2,1,0:T(1,128)S(1)}, u32[]{:S(2)}) copy-start(s32[32,1,1]{2,1,0:T(1,128)S(1)} %all-to-all-done.1) | copy-start | bytes 388
  220.8 39.2 %all-to-all-start.5 = ((bf16[32,64,256]{2,1,0:T(8,128)(2,1)}), bf16[32,64,256]{2,1,0:T(8,128)(2,1)}, u32[]{:S(2)}, u32[]{:S(2)}) async-start(bf16[32,64,256]{2,1,0:T(8,128)(2,1)} %bitcast.104), calls=%async_computation.5 | async-start | bytes 2097152 | tf_op jit(solution)/shard_map/all_to_all | solution.py:107
  239.0 1.8 copy-start.6
  239.0 1.8 copy-start.10
  257.3 12.9 %copy-start.20 = (s32[256,8]{0,1:T(8,128)S(1)}, s32[256,8]{0,1:T(8,128)}, u32[]{:S(2)}) copy-start(s32[256,8]{0,1:T(8,128)} %get-tuple-element.14) | copy-start | bytes 24580
  257.3 13.2 %copy-start.19 = (s32[256,8]{0,1:T(8,128)S(1)}, s32[256,8]{0,1:T(8,128)}, u32[]{:S(2)}) copy-start(s32[256,8]{0,1:T(8,128)} %get-tuple-element.17) | copy-start | bytes 24580
  260.0 12.3 %copy-start.15 = (s32[32,1,1]{2,1,0:T(1,128)S(1)}, s32[32,1,1]{2,1,0:T(1,128)}, u32[]{:S(2)}) copy-start(s32[32,1,1]{2,1,0:T(1,128)} %copy-done.14) | copy-start | bytes 388
  260.0 13.6 %copy-start.13 = (s32[32,1,64]{2,1,0:T(1,128)S(1)}, s32[32,1,64]{2,1,0:T(1,128)}, u32[]{:S(2)}) copy-start(s32[32,1,64]{2,1,0:T(1,128)} %copy-done.12) | copy-start | bytes 24580
  260.0 339.7 %all-to-all-start.7 = ((bf16[32,64,256]{2,1,0:T(8,128)(2,1)}), bf16[32,64,256]{2,1,0:T(8,128)(2,1)}, u32[]{:S(2)}, u32[]{:S(2)}) async-start(bf16[32,64,256]{2,1,0:T(8,128)(2,1)} %bitcast.24), calls=%async_computation.7 | async-start | bytes 2097152 | tf_op jit(solution)/shard_map/all_to_all | solution.py:107
  269.9 315.6 %all-reduce.5.cloned.1.call-start = ((), (), s32[]{:S(2)}) async-start(), calls=%async_computation.9 | async-start | bytes 2097152 | tf_op jit(solution)/shard_map/psum | solution.py:128
  325.5 356.4 %all-reduce.3.cloned.1.call-start = ((), (), s32[]{:S(2)}) async-start(), calls=%async_computation.8 | async-start | bytes 2097152 | tf_op jit(solution)/shard_map/psum | solution.py:122
  611.9 3.5 copy-start.23
  611.9 4.1 copy-start.9
  616.1 67.8 %copy-start.22 = (f32[2048]{0:T(1024)S(1)}, f32[2048]{0:T(1024)}, u32[]{:S(2)}) copy-start(f32[2048]{0:T(1024)} %param.15) | copy-start | bytes 24580
  684.5 2.2 copy-start.11
Sparse Core Ops, SparseCore 0:
  325.6 259.8 all-reduce.4
Sparse Core Ops, SparseCore 1:
  615.5 66.3 all-reduce.2
where the time goes:
time: 702 us; the launch traced here: 696 us
  waiting for transfers between devices  329 us (47%)
  other arithmetic  133 us (19%)
  local copies, waits for them, and re-layouts  92.7 us (13%)
  starting transfers between devices  61.3 us (9%)
  blocking collectives  32.5 us (5%)
  matrix products  30.5 us (4%)
  between operations  16.3 us (2%)
    psum x1, waiting for transfers between devices, on_device(): total_hot = lax.psum(hot_grad, ('shard', 'dp'))  248 us
    psum x1, waiting for transfers between devices, on_device(): lax.psum(cold_grad.astype(jnp.bfloat16), 'dp').astype(jnp.float32)  64.7 us
    scatter-add x2, other arithmetic, on_device(): jax.ops.segment_sum(gradients[:, :cold_feats].reshape(-1, row_width), slo...  27.1 us
    scatter-add x2, other arithmetic, on_device(): jax.ops.segment_sum(gradients[:, cold_feats:].reshape(-1, row_width), hot...  25.5 us
    scatter-add x2, other arithmetic, on_device(): jax.ops.segment_sum(owner_grad.reshape(-1, row_width), requested.reshape(...  24.9 us
    scatter-add x2, other arithmetic, on_device(): jax.ops.segment_sum(live_mask.reshape(-1), requested.reshape(-1), num_seg...  22.6 us
    all_to_all x2, starting transfers between devices, on_device(): lax.all_to_all(counts[micro_index], 'shard', split_axis=0, concat_axis=0,...  20.6 us
    all_to_all x1, blocking collectives, on_device(): lax.all_to_all(asked_rows, 'shard', split_axis=0, concat_axis=0, tiled=True)  20 us
  transfers between devices with their start and end apart: 9, of which 3 were waited for; matrix products, arithmetic and copies ran while one was open for 33% of the time, Pallas kernels for 0%

commit v1 on v0

--- a/solution.py
+++ b/solution.py
@@ -125,7 +125,7 @@
     averaged = summed_grad / jnp.maximum(summed_hits, 1.0)[:, None]
     updated, cold_accum_out = adagrad_rows(cold_table.astype(jnp.float32), cold_accum, averaged)
     cold_out = requantize(updated, dither_bits, summed_hits > 0.5)
-    total_hot = lax.psum(hot_grad, ("shard", "dp"))
+    total_hot = lax.psum(lax.psum(hot_grad, "dp"), "shard")
     hot_out, hot_accum_out = adagrad_rows(hot_table, hot_accum, total_hot)
     return (cold_out, cold_accum_out, hot_out, hot_accum_out)
 

time: 702 us -> 634 us (0.903)
  waiting for transfers between devices: 329 us -> 262 us
    psum x1 -> x2, waiting for transfers between devices: 248 us -> 180 us  [on_device(): total_hot = lax.psum(lax.psum(hot_grad, 'dp'), 'shard')]
  transfers between devices with their start and end apart: 9 -> 10, of which waited for: 3 -> 4; matrix products, arithmetic and copies ran while one was open for 33% -> 37% of each run, Pallas kernels for 0% -> 0%
where the time goes in v1:
time: 634 us; the launch traced here: 628 us
  waiting for transfers between devices  262 us (41%)
  other arithmetic  133 us (21%)
  local copies, waits for them, and re-layouts  92.7 us (15%)
  starting transfers between devices  61.2 us (10%)
  blocking collectives  33.7 us (5%)
  matrix products  30.5 us (5%)
  between operations  14.6 us (2%)
    psum x2, waiting for transfers between devices, on_device(): total_hot = lax.psum(lax.psum(hot_grad, 'dp'), 'shard')  180 us
    psum x1, waiting for transfers between devices, on_device(): lax.psum(cold_grad.astype(jnp.bfloat16), 'dp').astype(jnp.float32)  64.7 us
    scatter-add x2, other arithmetic, on_device(): jax.ops.segment_sum(gradients[:, :cold_feats].reshape(-1, row_width), slo...  27.1 us
    scatter-add x2, other arithmetic, on_device(): jax.ops.segment_sum(gradients[:, cold_feats:].reshape(-1, row_width), hot...  25.5 us
    scatter-add x2, other arithmetic, on_device(): jax.ops.segment_sum(owner_grad.reshape(-1, row_width), requested.reshape(...  24.9 us
    scatter-add x2, other arithmetic, on_device(): jax.ops.segment_sum(live_mask.reshape(-1), requested.reshape(-1), num_seg...  22.6 us
    all_to_all x2, starting transfers between devices, on_device(): lax.all_to_all(counts[micro_index], 'shard', split_axis=0, concat_axis=0,...  20.6 us
    all_to_all x1, blocking collectives, on_device(): lax.all_to_all(asked_rows, 'shard', split_axis=0, concat_axis=0, tiled=True)  20 us
  transfers between devices with their start and end apart: 10, of which 4 were waited for; matrix products, arithmetic and copies ran while one was open for 37% of the time, Pallas kernels for 0%

profile of v1, /device:TPU:8, one launch (start us, length us, event | category | flops | bytes accessed | tf_op | source)
XLA Modules:
  0.0 627.8 jit_solution(10525574304037473116)
XLA Ops:
  7.2 1.4 fusion.31
  8.6 20.0 %all_to_all.62 = s32[32,1,64]{2,1,0:T(1,128)S(1)} all-to-all(s32[32,1,64]{2,1,0:T(1,128)S(1)} %bitcast.113), channel_id=1, replica_groups=mesh['shard'=32,'dp'=8] {'shard'}, dimensions={0} | all-to-all | bytes 16384 | tf_op jit(solution)/shard_map/all_to_all | solution.py:82
  28.6 4.9 all-to-all-start
  33.6 9.9 %gather_fusion.3 = bf16[2048,256]{1,0:T(8,128)(2,1)} fusion(bf16[2048,256]{1,0:T(8,128)(2,1)} %param.14, s32[2048]{0:T(1024)S(1)} %broadcast_clamp_fusion.3), kind=kCustom, calls=%fused_computation.3 | custom fusion | bytes 2105344 | tf_op jit(solution)/shard_map/gather | solution.py:84
  43.5 10.0 %all-to-all-start.6 = ((bf16[32,64,256]{2,1,0:T(8,128)(2,1)}), bf16[32,64,256]{2,1,0:T(8,128)(2,1)S(1)}, u32[]{:S(2)}, u32[]{:S(2)}) async-start(bf16[32,64,256]{2,1,0:T(8,128)(2,1)} %bitcast.16), calls=%async_computation.6 | async-start | bytes 2097152 | tf_op jit(solution)/shard_map/all_to_all | solution.py:83
  53.6 9.1 %gather_fusion = bf16[2048,256]{1,0:T(8,128)(2,1)} fusion(bf16[2048,256]{1,0:T(8,128)(2,1)S(1)} %copy-done.2, s32[2048]{0:T(1024)S(1)} %broadcast_clamp_fusion.5), kind=kCustom, calls=%fused_computation | custom fusion | bytes 2105344 | tf_op jit(solution)/shard_map/gather | solution.py:84
  62.7 17.2 %all-to-all-done.6 = bf16[32,64,256]{2,1,0:T(8,128)(2,1)S(1)} async-done(((bf16[32,64,256]{2,1,0:T(8,128)(2,1)}), bf16[32,64,256]{2,1,0:T(8,128)(2,1)S(1)}, u32[]{:S(2)}, u32[]{:S(2)}) %all-to-all-start.6) | async-done | bytes 1048608 | tf_op jit(solution)/shard_map/all_to_all | solution.py:83
  79.9 5.6 all-to-all-start.4
  87.5 0.8 copy.69
  92.1 1.3 fusion.32
  93.5 0.8 copy.70
  97.2 8.4 %gather_fusion.5 = bf16[2048,256]{1,0:T(8,128)(2,1)} fusion(f32[1024,256]{1,0:T(8,128)S(1)} %copy-done.1, s32[2048]{0:T(1024)S(1)} %broadcast_clamp_fusion), kind=kCustom, calls=%fused_computation.5 | custom fusion | bytes 2105344 | tf_op jit(solution)/shard_map/gather | solution.py:90
  105.7 8.5 %gather_fusion.2 = bf16[2048,256]{1,0:T(8,128)(2,1)} fusion(f32[1024,256]{1,0:T(8,128)S(1)} %copy-done.1, s32[2048]{0:T(1024)S(1)} %broadcast_clamp_fusion.1), kind=kCustom, calls=%fused_computation.2 | custom fusion | bytes 2105344 | tf_op jit(solution)/shard_map/gather | solution.py:90
  114.2 9.0 %gather_fusion.4 = bf16[2048,256]{1,0:T(8,128)(2,1)} fusion(bf16[2048,256]{1,0:T(8,128)(2,1)S(1)} %bitcast.86, s32[2048]{0:T(1024)S(1)} %broadcast_clamp_fusion.2), kind=kCustom, calls=%fused_computation.4 | custom fusion | bytes 2105344 | tf_op jit(solution)/shard_map/gather | solution.py:89
  123.2 4.4 fusion.27
  127.6 1.5 pad_maximum_fusion.1
  129.1 10.5 %all-to-all-start.3 = ((s32[32,1,1]{2,1,0:T(1,128)}), s32[32,1,1]{2,1,0:T(1,128)}, u32[]{:S(2)}, u32[]{:S(2)}) async-start(s32[32,1,1]{2,1,0:T(1,128)} %copy.67), calls=%async_computation.3 | async-start | bytes 32768 | tf_op jit(solution)/shard_map/all_to_all | solution.py:110
  139.6 9.9 %gather_fusion.1 = bf16[2048,256]{1,0:T(8,128)(2,1)} fusion(bf16[2048,256]{1,0:T(8,128)(2,1)} %bitcast.6, s32[2048]{0:T(1024)S(1)} %broadcast_clamp_fusion.4), kind=kCustom, calls=%fused_computation.1 | custom fusion | bytes 2105344 | tf_op jit(solution)/shard_map/gather | solution.py:89
  149.5 4.3 fusion.28
  153.8 1.5 pad_maximum_fusion
  155.4 3.2 copy.77
  158.5 1.0 multiply_convert_fusion.2
  159.5 3.9 copy.84
  163.4 3.2 copy.71
  166.6 1.0 multiply_convert_fusion.3
  167.6 2.7 copy.82
  170.4 2.8 fusion.37
  173.2 1.2 fusion.34
  175.5 1.0 multiply_convert_fusion
  176.8 3.2 fusion.35
  180.1 1.9 copy.73
  182.0 5.9 copy.83
  187.9 10.1 %all-to-all-start.1 = ((s32[32,1,1]{2,1,0:T(1,128)}), s32[32,1,1]{2,1,0:T(1,128)S(1)}, u32[]{:S(2)}, u32[]{:S(2)}) async-start(s32[32,1,1]{2,1,0:T(1,128)} %copy.66), calls=%async_computation.1 | async-start | bytes 32768 | tf_op jit(solution)/shard_map/all_to_all | solution.py:110
  198.0 5.8 bitcast_add_fusion.1
  203.7 13.5 %scatter_custom_fusion.2 = f32[2048,256]{1,0:T(8,128)} fusion(s32[2048]{0:T(1024)} %reshape.252, f32[256,16,256]{2,1,0:T(8,128)} %bitcast_add_fusion.1, f32[]{:T(128)} %constant.13.clone.1), kind=kCustom, calls=%fused_computation.25 | custom fusion | flops 524288 | bytes 4194816 | tf_op jit(solution)/shard_map/scatter-add | solution.py:94
  217.2 2.7 convert_element_type.84
  219.9 9.8 %all-to-all-start.5 = ((bf16[32,64,256]{2,1,0:T(8,128)(2,1)}), bf16[32,64,256]{2,1,0:T(8,128)(2,1)}, u32[]{:S(2)}, u32[]{:S(2)}) async-start(bf16[32,64,256]{2,1,0:T(8,128)(2,1)} %bitcast.104), calls=%async_computation.5 | async-start | bytes 2097152 | tf_op jit(solution)/shard_map/all_to_all | solution.py:107
  229.8 0.8 copy.74
  231.3 1.2 fusion.39
  232.7 1.9 copy.79
  234.5 3.6 fusion.38
  238.1 1.8 copy.85
  239.9 2.9 bitcast_add_fusion
  242.8 13.6 %scatter_custom_fusion.4 = f32[2048,256]{1,0:T(8,128)} fusion(s32[2048]{0:T(1024)} %reshape.268, f32[256,16,256]{2,1,0:T(8,128)} %bitcast_add_fusion, f32[]{:T(128)} %constant.13.clone.1), kind=kCustom, calls=%fused_computation.23 | custom fusion | flops 524288 | bytes 4194816 | tf_op jit(solution)/shard_map/scatter-add | solution.py:94
  256.4 2.7 convert_element_type.90
  259.1 9.8 %all-to-all-start.7 = ((bf16[32,64,256]{2,1,0:T(8,128)(2,1)}), bf16[32,64,256]{2,1,0:T(8,128)(2,1)}, u32[]{:S(2)}, u32[]{:S(2)}) async-start(bf16[32,64,256]{2,1,0:T(8,128)(2,1)} %bitcast.24), calls=%async_computation.7 | async-start | bytes 2097152 | tf_op jit(solution)/shard_map/all_to_all | solution.py:107
  269.7 12.4 %scatter_custom_fusion.6 = f32[1024,256]{1,0:T(8,128)S(1)} fusion(s32[2048]{0:T(1024)S(1)} %reshape.284, f32[256,16,256]{2,1,0:T(8,128)} %bitcast_add_fusion.1, f32[]{:T(128)} %constant.13.clone.1), kind=kCustom, calls=%fused_computation.21 | custom fusion | flops 524288 | bytes 3146240 | tf_op jit(solution)/shard_map/scatter-add | solution.py:99
  282.1 13.1 %scatter_custom_fusion.7 = f32[1024,256]{1,0:T(8,128)} fusion(s32[2048]{0:T(1024)S(1)} %reshape.292, f32[256,16,256]{2,1,0:T(8,128)} %bitcast_add_fusion, f32[]{:T(128)} %constant.13.clone.1), kind=kCustom, calls=%fused_computation.19 | custom fusion | flops 524288 | bytes 3146240 | tf_op jit(solution)/shard_map/scatter-add | solution.py:99
  295.2 2.3 add.150
  297.6 1.4 reduce.3
  299.0 67.3 %all-reduce.6.cloned.1.call-done = f32[1024,256]{1,0:T(8,128)} async-done(((f32[1024,256]{1,0:T(8,128)}), f32[1024,256]{1,0:T(8,128)}) %all-reduce.6.cloned.1.call-update) | async-done | bytes 1048592 | tf_op jit(solution)/shard_map/psum | solution.py:128
  369.4 11.3 %scatter_custom_fusion.1 = f32[2048]{0:T(1024)S(1)} fusion(s32[2048]{0:T(1024)S(1)} %reshape.244, f32[2048]{0:T(1024)S(1)} %reshape.246, f32[]{:T(128)} %constant.13.clone.1), kind=kCustom, calls=%fused_computation.87 | custom fusion | flops 2048 | bytes 8196 | tf_op jit(solution)/shard_map/scatter-add | solution.py:118
  380.7 11.3 %scatter_custom_fusion = f32[2048]{0:T(1024)S(1)} fusion(s32[2048]{0:T(1024)S(1)} %reshape.236, f32[2048]{0:T(1024)S(1)} %reshape.238, f32[]{:T(128)} %constant.13.clone.1), kind=kCustom, calls=%fused_computation.89 | custom fusion | flops 2048 | bytes 8196 | tf_op jit(solution)/shard_map/scatter-add | solution.py:118
  392.0 13.7 %psum.28 = bf16[2048]{0:T(1024)(128)(2,1)S(1)} all-reduce(bf16[2048]{0:T(1024)(128)(2,1)S(1)} %add_convert_fusion.1), channel_id=1, replica_groups=mesh['shard'=32,'dp'=8] {'dp'}, use_global_device_ids=true, to_apply=%region_2.0 | all-reduce | flops 2048 | bytes 8192 | tf_op jit(solution)/shard_map/psum | solution.py:123
  405.7 112.6 %all-reduce.8.cloned.1.call-done = f32[1024,256]{1,0:T(8,128)} async-done(((f32[1024,256]{1,0:T(8,128)}), f32[1024,256]{1,0:T(8,128)}) %all-reduce.8.cloned.1.call-update) | async-done | bytes 1048592 | tf_op jit(solution)/shard_map/psum | solution.py:128
  518.3 1.4 multiply_reduce_fusion.1
  519.8 12.6 %scatter_custom_fusion.3 = f32[2048,256]{1,0:T(8,128)} fusion(s32[2048]{0:T(1024)S(1)} %reshape.236, bf16[2048,256]{1,0:T(8,128)(2,1)} %bitcast.28, f32[]{:T(128)} %constant.13.clone.1), kind=kCustom, calls=%fused_computation.30 | custom fusion | flops 1048576 | bytes 3145732 | tf_op jit(solution)/shard_map/scatter-add | solution.py:112
  532.4 12.3 %scatter_custom_fusion.5 = f32[2048,256]{1,0:T(8,128)} fusion(s32[2048]{0:T(1024)S(1)} %reshape.244, bf16[2048,256]{1,0:T(8,128)(2,1)} %bitcast.29, f32[]{:T(128)} %constant.13.clone.1), kind=kCustom, calls=%fused_computation.28 | custom fusion | flops 1048576 | bytes 3145732 | tf_op jit(solution)/shard_map/scatter-add | solution.py:112
  544.7 3.5 add_convert_fusion
  548.9 1.2 divide_subtract_fusion.1
  550.0 64.7 %all-reduce.4.cloned.1.call-done = bf16[2048,256]{1,0:T(8,128)(2,1)} async-done(((bf16[2048,256]{1,0:T(8,128)(2,1)}), bf16[2048,256]{1,0:T(8,128)(2,1)}) %all-reduce.4.cloned.1.call-update) | async-done | bytes 1048592 | tf_op jit(solution)/shard_map/psum | solution.py:122
  614.7 1.9 multiply_reduce_fusion
  617.2 2.2 abs_reduce_fusion
  619.5 1.5 fusion
  (117 shorter events, 16.4 us)
Async XLA Ops:
  7.2 167.3 %copy-start = (bf16[256,512]{1,0:T(8,128)(2,1)S(1)}, bf16[256,512]{1,0:T(8,128)(2,1)}, u32[]{:S(2)}) copy-start(bf16[256,512]{1,0:T(8,128)(2,1)} %param.20) | copy-start | bytes 786436
  28.6 14.9 %copy-start.12 = (s32[32,1,64]{2,1,0:T(1,128)}, s32[32,1,64]{2,1,0:T(1,128)S(1)}, u32[]{:S(2)}) copy-start(s32[32,1,64]{2,1,0:T(1,128)S(1)} %all_to_all.62) | copy-start | bytes 24580
  28.6 14.9 %all-to-all-start = ((s32[32,1,64]{2,1,0:T(1,128)}), s32[32,1,64]{2,1,0:T(1,128)S(1)}, u32[]{:S(2)}, u32[]{:S(2)}) async-start(s32[32,1,64]{2,1,0:T(1,128)} %bitcast), calls=%async_computation | async-start | bytes 32768 | tf_op jit(solution)/shard_map/all_to_all | solution.py:82
  43.5 10.1 %copy-start.2 = (bf16[2048,256]{1,0:T(8,128)(2,1)S(1)}, bf16[2048,256]{1,0:T(8,128)(2,1)}, u32[]{:S(2)}) copy-start(bf16[2048,256]{1,0:T(8,128)(2,1)} %param.14) | copy-start | bytes 3145732
  43.5 36.4 %all-to-all-start.6 = ((bf16[32,64,256]{2,1,0:T(8,128)(2,1)}), bf16[32,64,256]{2,1,0:T(8,128)(2,1)S(1)}, u32[]{:S(2)}, u32[]{:S(2)}) async-start(bf16[32,64,256]{2,1,0:T(8,128)(2,1)} %bitcast.16), calls=%async_computation.6 | async-start | bytes 2097152 | tf_op jit(solution)/shard_map/all_to_all | solution.py:83
  62.7 22.8 %copy-start.27 = (s32[2,32]{1,0:T(2,128)S(1)}, s32[2,32]{1,0:T(2,128)}, u32[]{:S(2)}) copy-start(s32[2,32]{1,0:T(2,128)} %param.27) | copy-start | bytes 772
  62.7 24.2 %copy-start.21 = (s32[512,8]{0,1:T(8,128)S(1)}, s32[512,8]{0,1:T(8,128)}, u32[]{:S(2)}) copy-start(s32[512,8]{0,1:T(8,128)} %param.25) | copy-start | bytes 49156
  62.7 34.5 %copy-start.1 = (f32[1024,256]{1,0:T(8,128)S(1)}, f32[1024,256]{1,0:T(8,128)}, u32[]{:S(2)}) copy-start(f32[1024,256]{1,0:T(8,128)} %param.17) | copy-start | bytes 3145732
  79.9 49.2 %all-to-all-start.4 = ((bf16[32,64,256]{2,1,0:T(8,128)(2,1)}), bf16[32,64,256]{2,1,0:T(8,128)(2,1)}, u32[]{:S(2)}, u32[]{:S(2)}) async-start(bf16[32,64,256]{2,1,0:T(8,128)(2,1)} %bitcast.103), calls=%async_computation.4 | async-start | bytes 2097152 | tf_op jit(solution)/shard_map/all_to_all | solution.py:83
  97.2 8.4 %copy-start.18 = (s32[2048]{0:T(1024)S(1)}, s32[2048]{0:T(1024)}, u32[]{:S(2)}) copy-start(s32[2048]{0:T(1024)} %reshape.204) | copy-start | bytes 24580
  105.7 8.5 %copy-start.16 = (s32[2048]{0:T(1024)S(1)}, s32[2048]{0:T(1024)}, u32[]{:S(2)}) copy-start(s32[2048]{0:T(1024)} %reshape.196) | copy-start | bytes 24580
  105.7 8.5 %copy-start.17 = (s32[2048]{0:T(1024)S(1)}, s32[2048]{0:T(1024)}, u32[]{:S(2)}) copy-start(s32[2048]{0:T(1024)} %reshape.220) | copy-start | bytes 24580
  123.2 4.4 copy-start.4
  123.2 4.4 copy-start.5
  129.1 58.8 %all-to-all-start.3 = ((s32[32,1,1]{2,1,0:T(1,128)}), s32[32,1,1]{2,1,0:T(1,128)}, u32[]{:S(2)}, u32[]{:S(2)}) async-start(s32[32,1,1]{2,1,0:T(1,128)} %copy.67), calls=%async_computation.3 | async-start | bytes 32768 | tf_op jit(solution)/shard_map/all_to_all | solution.py:110
  149.5 4.3 copy-start.7
  149.5 4.3 copy-start.8
  167.6 2.8 copy-start.3
  173.2 1.3 copy-start.24
  173.2 1.5 copy-start.25
  174.8 0.7 copy-start.26
  187.9 32.0 %all-to-all-start.1 = ((s32[32,1,1]{2,1,0:T(1,128)}), s32[32,1,1]{2,1,0:T(1,128)S(1)}, u32[]{:S(2)}, u32[]{:S(2)}) async-start(s32[32,1,1]{2,1,0:T(1,128)} %copy.66), calls=%async_computation.1 | async-start | bytes 32768 | tf_op jit(solution)/shard_map/all_to_all | solution.py:110
  219.9 9.8 %copy-start.14 = (s32[32,1,1]{2,1,0:T(1,128)}, s32[32,1,1]{2,1,0:T(1,128)S(1)}, u32[]{:S(2)}) copy-start(s32[32,1,1]{2,1,0:T(1,128)S(1)} %all-to-all-done.1) | copy-start | bytes 388
  219.9 39.2 %all-to-all-start.5 = ((bf16[32,64,256]{2,1,0:T(8,128)(2,1)}), bf16[32,64,256]{2,1,0:T(8,128)(2,1)}, u32[]{:S(2)}, u32[]{:S(2)}) async-start(bf16[32,64,256]{2,1,0:T(8,128)(2,1)} %bitcast.104), calls=%async_computation.5 | async-start | bytes 2097152 | tf_op jit(solution)/shard_map/all_to_all | solution.py:107
  238.1 1.8 copy-start.6
  238.1 1.8 copy-start.10
  256.4 12.8 %copy-start.20 = (s32[256,8]{0,1:T(8,128)S(1)}, s32[256,8]{0,1:T(8,128)}, u32[]{:S(2)}) copy-start(s32[256,8]{0,1:T(8,128)} %get-tuple-element.14) | copy-start | bytes 24580
  256.4 13.1 %copy-start.19 = (s32[256,8]{0,1:T(8,128)S(1)}, s32[256,8]{0,1:T(8,128)}, u32[]{:S(2)}) copy-start(s32[256,8]{0,1:T(8,128)} %get-tuple-element.17) | copy-start | bytes 24580
  259.1 273.3 %all-to-all-start.7 = ((bf16[32,64,256]{2,1,0:T(8,128)(2,1)}), bf16[32,64,256]{2,1,0:T(8,128)(2,1)}, u32[]{:S(2)}, u32[]{:S(2)}) async-start(bf16[32,64,256]{2,1,0:T(8,128)(2,1)} %bitcast.24), calls=%async_computation.7 | async-start | bytes 2097152 | tf_op jit(solution)/shard_map/all_to_all | solution.py:107
  269.0 97.4 %all-reduce.6.cloned.1.call-start = ((), (), s32[]{:S(2)}) async-start(), calls=%async_computation.9 | async-start | bytes 2097152 | tf_op jit(solution)/shard_map/psum | solution.py:128
  295.2 71.4 %copy-start.15 = (s32[32,1,1]{2,1,0:T(1,128)S(1)}, s32[32,1,1]{2,1,0:T(1,128)}, u32[]{:S(2)}) copy-start(s32[32,1,1]{2,1,0:T(1,128)} %copy-done.14) | copy-start | bytes 388
  295.2 72.7 %copy-start.13 = (s32[32,1,64]{2,1,0:T(1,128)S(1)}, s32[32,1,64]{2,1,0:T(1,128)}, u32[]{:S(2)}) copy-start(s32[32,1,64]{2,1,0:T(1,128)} %copy-done.12) | copy-start | bytes 24580
  297.6 220.8 %all-reduce.8.cloned.1.call-start = ((), (), s32[]{:S(2)}) async-start(), calls=%async_computation.10 | async-start | bytes 2097152 | tf_op jit(solution)/shard_map/psum | solution.py:128
  366.4 248.4 %all-reduce.4.cloned.1.call-start = ((), (), s32[]{:S(2)}) async-start(), calls=%async_computation.8 | async-start | bytes 2097152 | tf_op jit(solution)/shard_map/psum | solution.py:122
  544.7 3.5 copy-start.23
  544.7 4.1 copy-start.9
  548.9 67.8 %copy-start.22 = (f32[2048]{0:T(1024)S(1)}, f32[2048]{0:T(1024)}, u32[]{:S(2)}) copy-start(f32[2048]{0:T(1024)} %param.15) | copy-start | bytes 24580
  617.2 2.2 copy-start.11
Sparse Core Ops, SparseCore 0:
  297.7 68.5 all-reduce.5
  369.8 148.5 all-reduce.7
  548.4 66.3 all-reduce.3
